TPU v7x, 256 devices: a whole 4x4x8 slice. The times are simulated.
256 devices in a mesh: ctx: 64 (over y, z, core), head: 4 (over x).
Axes of the slice: x: 4, y: 4, z: 8, core: 2. Of those that a mesh axis runs over, the one named last changes fastest.
Arguments:
- query: bfloat16 [64, 2, 512, 4096], P('ctx', None, None, 'head'), may hold values from -48 to 48
- key: bfloat16 [64, 2, 512, 512], P('ctx', None, 'head'), may hold values from -18 to 18
- value: bfloat16 [64, 2, 512, 512], P('ctx', None, 'head'), may hold values from -6 to 6
- d_out: bfloat16 [64, 2, 512, 4096], P('ctx', None, None, 'head'), may hold values from -6 to 6
- doc_start: int32 [512], replicated, may hold values from 0 to 1, as said below
Outputs:
- d_query: bfloat16 [64, 2, 512, 4096], P('ctx', None, None, 'head')
- d_key: bfloat16 [64, 2, 512, 512], P('ctx', None, 'head')
- d_value: bfloat16 [64, 2, 512, 512], P('ctx', None, 'head')
Inputs may be any that keep to these rules, and one draw needn't show every extreme that they name: `doc_start`: 1 where a document begins at that block of 128 tokens (blocks in sequence order); block 0 begins one; from every beginning the next beginning, or the end of the sequence, is 1 to 3 blocks away; the first block of every span after the first lies inside a document of exactly 3 blocks that began in the span before.
All inputs are finite; a program needn't handle non-finite values.
Results may differ from a plain program's by a relative error of at most 0.039.
Values may be sent and summed in bfloat16 or wider, within the bound.
A program may use at most 64 MiB of HBM per device.

v0:
```python
import jax
import jax.numpy as jnp
from jax import lax
from jax.sharding import PartitionSpec as P

HD = 128
BLK = 128
GROUP = 8


def padded_2(cells, sides, width):
    for axis, dim in sides:
        count = lax.axis_size(axis)
        ends = count - 1
        head = lax.slice_in_dim(cells, 0, width, axis=dim)
        tail = lax.slice_in_dim(cells, cells.shape[dim] - width, cells.shape[dim], axis=dim)
        cells = jnp.concatenate(
            [
                lax.ppermute(tail, axis, [(i, (i + 1) % count) for i in range(ends)]),
                cells,
                lax.ppermute(head, axis, [((i + 1) % count, i) for i in range(ends)]),
            ],
            axis=dim,
        )
    return cells


def windowed(extended, reach_rows, blocks):
    pieces = []
    for offset in range(reach_rows // BLK + 1):
        sliced = lax.slice_in_dim(extended, offset * BLK, offset * BLK + blocks * BLK, axis=0)
        pieces.append(sliced.reshape((blocks, BLK) + extended.shape[1:]))
    return jnp.concatenate(pieces, axis=1)


def unwindowed(windows, reach_rows, blocks):
    summed = None
    for offset in range(reach_rows // BLK + 1):
        sliced = windows[:, offset * BLK : (offset + 1) * BLK].reshape(
            (blocks * BLK,) + windows.shape[2:]
        )
        padded = jnp.pad(
            sliced, ((offset * BLK, reach_rows - offset * BLK),) + ((0, 0),) * (windows.ndim - 2)
        )
        summed = padded if summed is None else summed + padded
    return summed


def span_grads(queries, grads_out, keys_ext, values_ext, doc_begins, span_start, reach_rows):
    blocks = queries.shape[0] // BLK
    kv_heads = keys_ext.shape[1] // HD
    score_scale = HD ** (-0.5)
    q_blocks = queries.reshape(blocks, BLK, kv_heads, GROUP, HD)
    do_blocks = grads_out.reshape(blocks, BLK, kv_heads, GROUP, HD)
    k_windows = windowed(keys_ext.reshape(-1, kv_heads, HD), reach_rows, blocks)
    v_windows = windowed(values_ext.reshape(-1, kv_heads, HD), reach_rows, blocks)
    row_pos = jnp.arange(BLK, dtype=jnp.int32)[None, :, None]
    col_pos = jnp.arange(reach_rows + BLK, dtype=jnp.int32)[None, None, :]
    key_pos = (
        span_start - reach_rows + jnp.arange(blocks, dtype=jnp.int32)[:, None, None] * BLK + col_pos
    )
    visible = (col_pos <= row_pos + reach_rows) & (key_pos >= doc_begins[:, None, None])
    visible = visible[:, None, None]
    scores = (
        jnp.einsum("btgjd,bkgd->bgjtk", q_blocks, k_windows, preferred_element_type=jnp.float32)
        * score_scale
    )
    peak = jnp.max(jnp.where(visible, scores, -1e30), axis=-1, keepdims=True)
    weights = jnp.exp(jnp.where(visible, scores - peak, -1e30))
    probs = weights / jnp.sum(weights, axis=-1, keepdims=True)
    probs_b = probs.astype(jnp.bfloat16)
    outputs = jnp.einsum(
        "bgjtk,bkgd->btgjd", probs_b, v_windows, preferred_element_type=jnp.float32
    ).astype(jnp.bfloat16)
    deltas = jnp.sum(do_blocks.astype(jnp.float32) * outputs.astype(jnp.float32), axis=-1)
    dprobs = jnp.einsum(
        "btgjd,bkgd->bgjtk", do_blocks, v_windows, preferred_element_type=jnp.float32
    )
    dscores = (
        probs * (dprobs - jnp.transpose(deltas, (0, 2, 3, 1))[..., None]) * score_scale
    ).astype(jnp.bfloat16)
    d_queries = jnp.einsum(
        "bgjtk,bkgd->btgjd", dscores, k_windows, preferred_element_type=jnp.float32
    ).astype(jnp.bfloat16)
    dk_windows = jnp.einsum(
        "bgjtk,btgjd->bkgd", dscores, q_blocks, preferred_element_type=jnp.float32
    )
    dv_windows = jnp.einsum(
        "bgjtk,btgjd->bkgd", probs_b, do_blocks, preferred_element_type=jnp.float32
    )
    return (
        d_queries.reshape(blocks * BLK, -1),
        unwindowed(dk_windows, reach_rows, blocks).reshape(-1, kv_heads * HD),
        unwindowed(dv_windows, reach_rows, blocks).reshape(-1, kv_heads * HD),
    )


def per_device(query, key, value, d_out, doc_start):
    kv_key, kv_value = (
        lax.all_to_all(key, "head", split_axis=3, concat_axis=2, tiled=True),
        lax.all_to_all(value, "head", split_axis=3, concat_axis=2, tiled=True),
    )
    span_rows = kv_key.shape[2]
    ctx_index = lax.axis_index("ctx")
    ctx_count = lax.axis_size("ctx")
    is_last = ctx_index == ctx_count - 1
    rim_from = span_rows - span_rows
    outgoing = jnp.stack(
        [
            jnp.stack([kv_key[0, 1, rim_from:], kv_value[0, 1, rim_from:]]),
            jnp.stack([kv_key[0, 0, rim_from:], kv_value[0, 0, rim_from:]]),
        ]
    )
    incoming = padded_2(outgoing, (("ctx", 0),), 1)
    previous = [incoming[0], jnp.where(is_last, outgoing[1], incoming[3])]
    run_begin = (
        lax.cummax(
            jnp.where(doc_start == 1, jnp.arange(doc_start.shape[0], dtype=jnp.int32), 0), axis=0
        )
        * BLK
    )
    blocks = span_rows // BLK
    span_results = []
    for span_slot in range(2):
        span_id = ctx_index if span_slot == 0 else 2 * ctx_count - 1 - ctx_index
        span_start = span_id * span_rows
        doc_begins = lax.dynamic_slice_in_dim(run_begin, span_id * blocks, blocks)
        keys_ext = jnp.concatenate([previous[span_slot][0], kv_key[0, span_slot]], axis=0)
        values_ext = jnp.concatenate([previous[span_slot][1], kv_value[0, span_slot]], axis=0)
        span_results.append(
            span_grads(
                query[0, span_slot],
                d_out[0, span_slot],
                keys_ext,
                values_ext,
                doc_begins,
                span_start,
                span_rows,
            )
        )
    partials = jnp.stack(
        [
            jnp.stack([span_results[0][1][:span_rows], span_results[0][2][:span_rows]]),
            jnp.stack([span_results[1][1][:span_rows], span_results[1][2][:span_rows]]),
        ]
    )
    returned = padded_2(partials.astype(jnp.bfloat16), (("ctx", 0),), 1).astype(partials.dtype)
    added_parts = [returned[3] + jnp.where(is_last, partials[1], 0.0), returned[0]]
    key_grads = []
    value_grads = []
    for span_slot in range(2):
        own_key = (
            span_results[span_slot][1][span_rows:].at[rim_from:].add(added_parts[span_slot][0])
        )
        own_value = (
            span_results[span_slot][2][span_rows:].at[rim_from:].add(added_parts[span_slot][1])
        )
        key_grads.append(own_key.astype(jnp.bfloat16))
        value_grads.append(own_value.astype(jnp.bfloat16))
    d_query = jnp.stack([span_results[0][0], span_results[1][0]])[None]
    key_layout = jnp.stack(key_grads)[None]
    value_layout = jnp.stack(value_grads)[None]
    d_key, d_value = (
        lax.all_to_all(key_layout, "head", split_axis=2, concat_axis=3, tiled=True),
        lax.all_to_all(value_layout, "head", split_axis=2, concat_axis=3, tiled=True),
    )
    return (d_query, d_key, d_value)


def solution(mesh):
    return jax.shard_map(
        per_device,
        mesh=mesh,
        in_specs=(
            P("ctx", None, None, "head"),
            P("ctx", None, "head", None),
            P("ctx", None, "head", None),
            P("ctx", None, None, "head"),
            P(),
        ),
        out_specs=(
            P("ctx", None, None, "head"),
            P("ctx", None, "head", None),
            P("ctx", None, "head", None),
        ),
        check_vma=False,
    )
```

profile of v0, /device:TPU:26, one launch (start us, length us, event | category | flops | bytes accessed | tf_op | source)
XLA Modules:
  0.0 143.1 jit_solution(6247647339542804097)
XLA Ops:
  0.6 1.8 %copy.44 = bf16[1,2,128,512]{2,1,0,3:T(2,128)(2,1)} copy(bf16[1,2,128,512]{3,2,1,0:T(8,128)(2,1)} %param.22) | data formatting | bytes 524288 | tf_op args[1]
  2.5 4.8 %all-to-all-start = ((bf16[1,2,128,512]{2,1,0,3:T(2,128)(2,1)}), bf16[1,2,128,512]{2,1,0,3:T(2,128)(2,1)S(1)}, u32[]{:S(2)}, u32[]{:S(2)}) async-start(bf16[1,2,128,512]{2,1,0,3:T(2,128)(2,1)} %copy.44), calls=%async_computation | async-start | bytes 524288 | tf_op jit(solution)/shard_map/all_to_all | solution.py:100
  8.6 1.8 %copy.46 = bf16[1,2,128,512]{2,1,0,3:T(2,128)(2,1)} copy(bf16[1,2,128,512]{3,2,1,0:T(8,128)(2,1)} %param.23) | data formatting | bytes 524288 | tf_op args[2]
  12.1 4.6 %slice_bitcast_fusion.3 = (bf16[64,8,8,128]{3,1,2,0:T(8,128)(2,1)}, f32[64,8,8,128]{3,1,2,0:T(8,128)}, f32[64,8,8,128]{3,1,2,0:T(8,128)}, bf16[64,8,8,128]{3,1,2,0:T(8,128)(2,1)}) fusion(bf16[1,2,512,1024]{3,2,1,0:T(8,128)(2,1)} %param.24), kind=kLoop, calls=%fused_computation.68 | loop fusion | flops 1048576 | bytes 8388608
  16.9 4.8 %all-to-all-start.1 = ((bf16[1,2,128,512]{2,1,0,3:T(2,128)(2,1)}), bf16[1,2,128,512]{2,1,0,3:T(2,128)(2,1)S(1)}, u32[]{:S(2)}, u32[]{:S(2)}) async-start(bf16[1,2,128,512]{2,1,0,3:T(2,128)(2,1)} %copy.46), calls=%async_computation.1 | async-start | bytes 524288 | tf_op jit(solution)/shard_map/all_to_all | solution.py:101
  22.5 4.3 %all-to-all-done.1 = bf16[1,2,128,512]{2,1,0,3:T(2,128)(2,1)S(1)} async-done(((bf16[1,2,128,512]{2,1,0,3:T(2,128)(2,1)}), bf16[1,2,128,512]{2,1,0,3:T(2,128)(2,1)S(1)}, u32[]{:S(2)}, u32[]{:S(2)}) %all-to-all-start.1) | async-done | bytes 262176 | tf_op jit(solution)/shard_map/all_to_all | solution.py:101
  28.8 5.4 %collective-permute-start.1 = (bf16[1,2,512,128]{3,2,1,0:T(8,128)(2,1)}, bf16[1,2,512,128]{3,2,1,0:T(8,128)(2,1)}, u32[]{:S(2)}, u32[]{:S(2)}) collective-permute-start(bf16[1,2,512,128]{3,2,1,0:T(8,128)(2,1)} %maximum_bitcast_fusion.1), channel_id=1, source_target_pairs={{4,0},{8,4},{12,8},{16,12},{20,16},{24,20},{28,24},{32,28},{36,32}... | collective-permute-start | bytes 786440 | tf_op jit(solution)/shard_map/ppermute | solution.py:21
  34.8 2.5 %copy.98 = bf16[64,8,8,128]{3,2,1,0:T(8,128)(2,1)} copy(bf16[64,8,8,128]{3,1,2,0:T(8,128)(2,1)} %get-tuple-element.83) | data formatting | bytes 2097152
  38.8 3.4 %copy.99 = f32[64,8,8,128]{3,2,1,0:T(8,128)} copy(f32[64,8,8,128]{3,1,2,0:T(8,128)} %get-tuple-element.84) | data formatting | bytes 4194304
  42.2 2.9 %copy.52 = f32[4,128,1,8,128]{1,4,3,0,2:T(8,128)} copy(f32[4,128,1,8,128]{4,3,2,1,0:T(8,128)} %bitcast.414) | data formatting | bytes 4194304 | tf_op jit(solution)/shard_map/convert_element_type | solution.py:75
  45.1 3.4 %copy.102 = f32[64,8,8,128]{3,2,1,0:T(8,128)} copy(f32[64,8,8,128]{3,1,2,0:T(8,128)} %get-tuple-element.85) | data formatting | bytes 4194304
  48.5 2.9 %copy.60 = f32[4,128,1,8,128]{1,4,3,0,2:T(8,128)} copy(f32[4,128,1,8,128]{4,3,2,1,0:T(8,128)} %bitcast.415) | data formatting | bytes 4194304 | tf_op jit(solution)/shard_map/convert_element_type | solution.py:75
  51.4 2.2 %broadcast_and_fusion.1 = (pred[4,128,640]{1,2,0:T(8,128)(4,1)S(1)}, pred[4,128,640]{1,2,0:T(8,128)(4,1)S(1)}) fusion(pred[4,640]{1,0:T(4,128)(4,1)S(1)} %get-tuple-element.162, pred[128,640]{0,1:T(8,128)(4,1)} %iota_compare_fusion, pred[4,640]{1,0:T(4,128)(4,1)S(1)} %get-tuple-element.161), kind=kLoop, calls=%fused_computation.78 | loop fusion | flops 655360 | bytes 742400 | tf_op jit(solution)/shard_map/and | solution.py:62
  53.6 1.8 %fusion.81 = (bf16[1,2,512,128]{3,2,1,0:T(8,128)(2,1)}, bf16[2,512,128]{2,1,0:T(8,128)(2,1)S(1)}) fusion(bf16[1,512,128]{2,1,0:T(8,128)(2,1)} %get-tuple-element.159, bf16[1,512,128]{2,1,0:T(8,128)(2,1)} %get-tuple-element.114, bf16[1,2,512,128]{3,2,1,0:T(8,128)(2,1)} %collective-permute-done.1, pred[]{:T(512)S(6)} %eq.11), kind=kLoop, calls=%fused_computation.125 | loop fusion | flops 262144 | bytes 1048577 | tf_op jit(solution)/shard_map/stack | solution.py:108
  55.4 2.1 %collective-permute-start = (bf16[1,2,512,128]{3,2,1,0:T(8,128)(2,1)}, bf16[1,2,512,128]{3,2,1,0:T(8,128)(2,1)}, u32[]{:S(2)}, u32[]{:S(2)}) collective-permute-start(bf16[1,2,512,128]{3,2,1,0:T(8,128)(2,1)} %get-tuple-element.135), channel_id=1, source_target_pairs={{0,4},{4,8},{8,12},{12,16},{16,20},{20,24},{24,28},{28,32},{32,36}... | collective-permute-start | bytes 786440 | tf_op jit(solution)/shard_map/ppermute | solution.py:19
  60.5 2.4 %fusion.15 = f32[4,8,128]{2,1,0:T(8,128)S(1)} fusion(f32[4,640,128,8]{2,1,3,0:T(8,128)S(1)} %get-tuple-element.152, f32[4,8,128]{2,1,0:T(8,128)S(1)} %get-tuple-element.151, pred[4,128,640]{1,2,0:T(8,128)(4,1)S(1)} %get-tuple-element.148), kind=kLoop, calls=%fused_computation.21 | loop fusion | flops 10481664 | bytes 10846208 | tf_op jit(solution)/shard_map/reduce_sum | solution.py:70
  62.9 3.1 %fusion.41 = f32[4,640,1,128]{3,1,0,2:T(8,128)S(1)} fusion(bf16[4,128,8,128]{3,2,1,0:T(8,128)(2,1)S(1)} %bitcast.439, f32[4,8,128]{2,1,0:T(8,128)S(1)} %fusion.15, f32[4,8,128]{2,1,0:T(8,128)S(1)} %get-tuple-element.151, f32[4,640,128,8]{2,1,3,0:T(8,128)S(1)} %get-tuple-element.152, pred[4,128,640]{1,2,0:T(8,128)(4,1)S(1)} %get-tuple-element.148), kind=kOutput, calls=%fused_computation.50 | convolution fusion | flops 684195840 | bytes 13205504 | tf_op jit(solution)/shard_map/bgjtk,btgjd->bkgd/dot_general | solution.py:88
  66.1 3.2 %fusion.29 = f32[4,128,8]{1,2,0:T(8,128)S(1)} fusion(f32[4,128,1,8,128]{1,4,3,0,2:T(8,128)S(1)} %copy-done.6, bf16[4,640,1,128]{3,1,0,2:T(8,128)(2,1)S(1)} %constant_dynamic-update-slice_fusion.15, f32[4,8,128]{2,1,0:T(8,128)S(1)} %fusion.15, f32[4,8,128]{2,1,0:T(8,128)S(1)} %get-tuple-element.151, f32[4,640,128,8]{2,1,3,0:T(8,128)S(1)} %get-tuple-element.152, ...), kind=kOutput, calls=%fused_computation.37 | convolution fusion | flops 686288896 | bytes 13615104 | tf_op jit(solution)/shard_map/bgjtk,bkgd->btgjd/dot_general | solution.py:72
  69.2 4.2 %fusion.17 = bf16[4,8,128,640]{2,3,1,0:T(8,128)(2,1)S(1)} fusion(f32[4,8,128]{2,1,0:T(8,128)S(1)} %bitcast.468, f32[4,8,128]{2,1,0:T(8,128)S(1)} %fusion.15, f32[4,8,128]{2,1,0:T(8,128)S(1)} %get-tuple-element.151, f32[4,640,128,8]{2,1,3,0:T(8,128)S(1)} %get-tuple-element.152, pred[4,128,640]{1,2,0:T(8,128)(4,1)S(1)} %get-tuple-element.148, ...), kind=kOutput, calls=%fused_computation.23 | convolution fusion | flops 692060160 | bytes 17809408 | tf_op jit(solution)/shard_map/btgjd,bkgd->bgjtk/dot_general | solution.py:76
  76.2 2.1 %collective-permute-start.2 = (bf16[1,2,512,128]{3,2,1,0:T(8,128)(2,1)S(1)}, bf16[1,2,512,128]{3,2,1,0:T(8,128)(2,1)S(1)}, u32[]{:S(2)}, u32[]{:S(2)}) collective-permute-start(bf16[1,2,512,128]{3,2,1,0:T(8,128)(2,1)S(1)} %fusion.76), channel_id=1, source_target_pairs={{0,4},{4,8},{8,12},{12,16},{16,20},{20,24},{24,28},{28,32},{32,36}... | collective-permute-start | bytes 786440 | tf_op jit(solution)/shard_map/ppermute | solution.py:19
  81.5 2.4 %fusion.13 = f32[4,8,128]{2,1,0:T(8,128)S(1)} fusion(f32[4,640,128,8]{2,1,3,0:T(8,128)S(1)} %get-tuple-element.154, f32[4,8,128]{2,1,0:T(8,128)S(1)} %get-tuple-element.153, pred[4,128,640]{1,2,0:T(8,128)(4,1)S(1)} %get-tuple-element.147), kind=kLoop, calls=%fused_computation.19 | loop fusion | flops 10481664 | bytes 10846208 | tf_op jit(solution)/shard_map/reduce_sum | solution.py:70
  83.9 4.2 %fusion.38 = f32[4,640,1,128]{3,1,0,2:T(8,128)S(1)} fusion(bf16[4,128,8,128]{3,2,1,0:T(8,128)(2,1)} %bitcast.437, f32[4,8,128]{2,1,0:T(8,128)S(1)} %fusion.13, f32[4,8,128]{2,1,0:T(8,128)S(1)} %get-tuple-element.153, f32[4,640,128,8]{2,1,3,0:T(8,128)S(1)} %get-tuple-element.154, pred[4,128,640]{1,2,0:T(8,128)(4,1)S(1)} %get-tuple-element.147), kind=kOutput, calls=%fused_computation.49 | convolution fusion | flops 684195840 | bytes 13205504 | tf_op jit(solution)/shard_map/bgjtk,btgjd->bkgd/dot_general | solution.py:88
  88.2 4.4 %fusion.31 = f32[4,128,8]{1,2,0:T(8,128)S(1)} fusion(f32[4,128,1,8,128]{1,4,3,0,2:T(8,128)S(1)} %copy-done.5, bf16[4,640,1,128]{3,1,0,2:T(8,128)(2,1)} %copy-done.14, f32[4,8,128]{2,1,0:T(8,128)S(1)} %fusion.13, f32[4,8,128]{2,1,0:T(8,128)S(1)} %get-tuple-element.153, f32[4,640,128,8]{2,1,3,0:T(8,128)S(1)} %get-tuple-element.154, ...), kind=kOutput, calls=%fused_computation.40 | convolution fusion | flops 686288896 | bytes 13615104 | tf_op jit(solution)/shard_map/bgjtk,bkgd->btgjd/dot_general | solution.py:72
  92.6 4.2 %fusion.16 = bf16[4,8,128,640]{2,3,1,0:T(8,128)(2,1)S(1)} fusion(f32[4,8,128]{2,1,0:T(8,128)S(1)} %bitcast.469, f32[4,8,128]{2,1,0:T(8,128)S(1)} %fusion.13, f32[4,8,128]{2,1,0:T(8,128)S(1)} %get-tuple-element.153, f32[4,640,128,8]{2,1,3,0:T(8,128)S(1)} %get-tuple-element.154, pred[4,128,640]{1,2,0:T(8,128)(4,1)S(1)} %get-tuple-element.147, ...), kind=kOutput, calls=%fused_computation.22 | convolution fusion | flops 692060160 | bytes 17809408 | tf_op jit(solution)/shard_map/btgjd,bkgd->bgjtk/dot_general | solution.py:76
  97.0 2.1 %copy-done = bf16[4,8,128,640]{2,3,1,0:T(8,128)(2,1)} copy-done((bf16[4,8,128,640]{2,3,1,0:T(8,128)(2,1)}, bf16[4,8,128,640]{2,3,1,0:T(8,128)(2,1)S(1)}, u32[]{:S(2)}) %copy-start) | copy-done | bytes 5242904
  101.7 6.0 %collective-permute-start.3 = (bf16[1,2,512,128]{3,2,1,0:T(8,128)(2,1)S(1)}, bf16[1,2,512,128]{3,2,1,0:T(8,128)(2,1)S(1)}, u32[]{:S(2)}, u32[]{:S(2)}) collective-permute-start(bf16[1,2,512,128]{3,2,1,0:T(8,128)(2,1)S(1)} %maximum_bitcast_fusion.2), channel_id=1, source_target_pairs={{4,0},{8,4},{12,8},{16,12},{20,16},{24,20},{28,24},{32,28},{36,32}... | collective-permute-start | bytes 786440 | tf_op jit(solution)/shard_map/ppermute | solution.py:21
  107.7 2.0 %fusion.45 = bf16[4,128,1,8,128]{1,4,3,0,2:T(8,128)(2,1)} fusion(bf16[4,8,128,640]{2,3,1,0:T(8,128)(2,1)S(1)} %fusion.17, bf16[4,640,1,128]{3,1,0,2:T(8,128)(2,1)S(1)} %constant_dynamic-update-slice_fusion.10), kind=kOutput, calls=%fused_computation.52 | convolution fusion | flops 671612928 | bytes 6946816 | tf_op jit(solution)/shard_map/bgjtk,bkgd->btgjd/dot_general | solution.py:82
  115.9 4.8 %all-to-all-start.3 = ((bf16[1,2,512,128]{3,1,0,2:T(2,128)(2,1)}), bf16[1,2,512,128]{3,1,0,2:T(2,128)(2,1)S(1)}, u32[]{:S(2)}, u32[]{:S(2)}) async-start(bf16[1,2,512,128]{3,1,0,2:T(2,128)(2,1)} %copy.71), calls=%async_computation.3 | async-start | bytes 524288 | tf_op jit(solution)/shard_map/all_to_all | solution.py:165
  123.5 2.5 %all-to-all-done.3 = bf16[1,2,512,128]{3,1,0,2:T(2,128)(2,1)S(1)} async-done(((bf16[1,2,512,128]{3,1,0,2:T(2,128)(2,1)}), bf16[1,2,512,128]{3,1,0,2:T(2,128)(2,1)S(1)}, u32[]{:S(2)}, u32[]{:S(2)}) %all-to-all-start.3) | async-done | bytes 262176 | tf_op jit(solution)/shard_map/all_to_all | solution.py:165
  126.0 4.8 %all-to-all-start.2 = ((bf16[1,2,512,128]{3,1,0,2:T(2,128)(2,1)}), bf16[1,2,512,128]{3,1,0,2:T(2,128)(2,1)S(1)}, u32[]{:S(2)}, u32[]{:S(2)}) async-start(bf16[1,2,512,128]{3,1,0,2:T(2,128)(2,1)} %maximum_bitcast_fusion.3), calls=%async_computation.2 | async-start | bytes 524288 | tf_op jit(solution)/shard_map/all_to_all | solution.py:164
  130.8 4.5 %fusion.44 = bf16[4,128,1,8,128]{1,4,3,0,2:T(8,128)(2,1)} fusion(bf16[4,8,128,640]{2,3,1,0:T(8,128)(2,1)} %copy-done, bf16[4,640,1,128]{3,1,0,2:T(8,128)(2,1)S(1)} %constant_dynamic-update-slice_fusion), kind=kOutput, calls=%fused_computation.51 | convolution fusion | flops 671612928 | bytes 6946816 | tf_op jit(solution)/shard_map/bgjtk,bkgd->btgjd/dot_general | solution.py:82
  138.3 2.7 %maximum_bitcast_fusion = bf16[1,2,512,1024]{3,2,1,0:T(8,128)(2,1)} fusion(bf16[1,512,1024]{2,1,0:T(8,128)(2,1)S(1)} %copy-done.1, bf16[1,512,1024]{2,1,0:T(8,128)(2,1)} %stack_reshape.6), kind=kLoop, calls=%fused_computation.34 | loop fusion | flops 1048576 | bytes 4194304 | tf_op jit(solution)/shard_map/broadcast_in_dim | solution.py:160
  (118 shorter events, 33.2 us)
Async XLA Ops:
  2.5 14.4 %all-to-all-start = ((bf16[1,2,128,512]{2,1,0,3:T(2,128)(2,1)}), bf16[1,2,128,512]{2,1,0,3:T(2,128)(2,1)S(1)}, u32[]{:S(2)}, u32[]{:S(2)}) async-start(bf16[1,2,128,512]{2,1,0,3:T(2,128)(2,1)} %copy.44), calls=%async_computation | async-start | bytes 524288 | tf_op jit(solution)/shard_map/all_to_all | solution.py:100
  16.9 10.0 %all-to-all-start.1 = ((bf16[1,2,128,512]{2,1,0,3:T(2,128)(2,1)}), bf16[1,2,128,512]{2,1,0,3:T(2,128)(2,1)S(1)}, u32[]{:S(2)}, u32[]{:S(2)}) async-start(bf16[1,2,128,512]{2,1,0,3:T(2,128)(2,1)} %copy.46), calls=%async_computation.1 | async-start | bytes 524288 | tf_op jit(solution)/shard_map/all_to_all | solution.py:101
  28.8 24.8 %collective-permute-start.1 = (bf16[1,2,512,128]{3,2,1,0:T(8,128)(2,1)}, bf16[1,2,512,128]{3,2,1,0:T(8,128)(2,1)}, u32[]{:S(2)}, u32[]{:S(2)}) collective-permute-start(bf16[1,2,512,128]{3,2,1,0:T(8,128)(2,1)} %maximum_bitcast_fusion.1), channel_id=1, source_target_pairs={{4,0},{8,4},{12,8},{16,12},{20,16},{24,20},{28,24},{32,28},{36,32}... | collective-permute-start | bytes 786440 | tf_op jit(solution)/shard_map/ppermute | solution.py:21
  55.4 23.0 %collective-permute-start = (bf16[1,2,512,128]{3,2,1,0:T(8,128)(2,1)}, bf16[1,2,512,128]{3,2,1,0:T(8,128)(2,1)}, u32[]{:S(2)}, u32[]{:S(2)}) collective-permute-start(bf16[1,2,512,128]{3,2,1,0:T(8,128)(2,1)} %get-tuple-element.135), channel_id=1, source_target_pairs={{0,4},{4,8},{8,12},{12,16},{16,20},{20,24},{24,28},{28,32},{32,36}... | collective-permute-start | bytes 786440 | tf_op jit(solution)/shard_map/ppermute | solution.py:19
  62.9 3.1 %copy-start.6 = (f32[4,128,1,8,128]{1,4,3,0,2:T(8,128)S(1)}, f32[4,128,1,8,128]{1,4,3,0,2:T(8,128)}, u32[]{:S(2)}) copy-start(f32[4,128,1,8,128]{1,4,3,0,2:T(8,128)} %copy.60) | copy-start | bytes 6291460
  73.5 6.0 %copy-start.11 = (bf16[512,128]{1,0:T(8,128)(2,1)S(1)}, bf16[512,128]{1,0:T(8,128)(2,1)}, u32[]{:S(2)}) copy-start(bf16[512,128]{1,0:T(8,128)(2,1)} %get-tuple-element.115) | copy-start | bytes 393220
  73.5 6.1 %copy-start.10 = (bf16[512,128]{1,0:T(8,128)(2,1)S(1)}, bf16[512,128]{1,0:T(8,128)(2,1)}, u32[]{:S(2)}) copy-start(bf16[512,128]{1,0:T(8,128)(2,1)} %get-tuple-element.158) | copy-start | bytes 393220
  73.6 6.1 %copy-start.13 = (bf16[1,1,512,128]{3,2,1,0:T(8,128)(2,1)S(1)}, bf16[1,1,512,128]{3,2,1,0:T(8,128)(2,1)}, u32[]{:S(2)}) copy-start(bf16[1,1,512,128]{3,2,1,0:T(8,128)(2,1)} %get-tuple-element.160) | copy-start | bytes 393220
  73.6 6.2 %copy-start.12 = (bf16[1,1,512,128]{3,2,1,0:T(8,128)(2,1)S(1)}, bf16[1,1,512,128]{3,2,1,0:T(8,128)(2,1)}, u32[]{:S(2)}) copy-start(bf16[1,1,512,128]{3,2,1,0:T(8,128)(2,1)} %get-tuple-element.113) | copy-start | bytes 393220
  76.1 5.4 %copy-start.2 = (f32[1,512,128]{2,1,0:T(8,128)}, f32[1,512,128]{2,1,0:T(8,128)S(1)}, u32[]{:S(2)}) copy-start(f32[1,512,128]{2,1,0:T(8,128)S(1)} %get-tuple-element.111) | copy-start | bytes 786436
  76.2 5.4 %copy-start.4 = (f32[1024,1,128]{2,0,1:T(8,128)}, f32[1024,1,128]{2,0,1:T(8,128)S(1)}, u32[]{:S(2)}) copy-start(f32[1024,1,128]{2,0,1:T(8,128)S(1)} %pad_add_fusion.1) | copy-start | bytes 1572868
  76.2 36.5 %collective-permute-start.2 = (bf16[1,2,512,128]{3,2,1,0:T(8,128)(2,1)S(1)}, bf16[1,2,512,128]{3,2,1,0:T(8,128)(2,1)S(1)}, u32[]{:S(2)}, u32[]{:S(2)}) collective-permute-start(bf16[1,2,512,128]{3,2,1,0:T(8,128)(2,1)S(1)} %fusion.76), channel_id=1, source_target_pairs={{0,4},{4,8},{8,12},{12,16},{16,20},{20,24},{24,28},{28,32},{32,36}... | collective-permute-start | bytes 786440 | tf_op jit(solution)/shard_map/ppermute | solution.py:19
  79.7 4.2 %copy-start.14 = (bf16[4,640,1,128]{3,1,0,2:T(8,128)(2,1)}, bf16[4,640,1,128]{3,1,0,2:T(8,128)(2,1)S(1)}, u32[]{:S(2)}) copy-start(bf16[4,640,1,128]{3,1,0,2:T(8,128)(2,1)S(1)} %constant_dynamic-update-slice_fusion.5) | copy-start | bytes 1966084
  83.9 4.2 %copy-start.5 = (f32[4,128,1,8,128]{1,4,3,0,2:T(8,128)S(1)}, f32[4,128,1,8,128]{1,4,3,0,2:T(8,128)}, u32[]{:S(2)}) copy-start(f32[4,128,1,8,128]{1,4,3,0,2:T(8,128)} %copy.52) | copy-start | bytes 6291460
  88.2 4.4 %copy-start.9 = (bf16[64,8,8,128]{3,2,1,0:T(8,128)(2,1)S(1)}, bf16[64,8,8,128]{3,2,1,0:T(8,128)(2,1)}, u32[]{:S(2)}) copy-start(bf16[64,8,8,128]{3,2,1,0:T(8,128)(2,1)} %copy.98) | copy-start | bytes 3145732
  88.2 4.4 %copy-start.15 = (bf16[4,640,1,128]{3,1,0,2:T(8,128)(2,1)S(1)}, bf16[4,640,1,128]{3,1,0,2:T(8,128)(2,1)}, u32[]{:S(2)}) copy-start(bf16[4,640,1,128]{3,1,0,2:T(8,128)(2,1)} %copy-done.14) | copy-start | bytes 1966084
  96.8 2.3 %copy-start = (bf16[4,8,128,640]{2,3,1,0:T(8,128)(2,1)}, bf16[4,8,128,640]{2,3,1,0:T(8,128)(2,1)S(1)}, u32[]{:S(2)}) copy-start(bf16[4,8,128,640]{2,3,1,0:T(8,128)(2,1)S(1)} %fusion.16) | copy-start | bytes 15728644
  97.0 10.7 %copy-start.7 = (f32[1024,1,128]{2,0,1:T(8,128)}, f32[1024,1,128]{2,0,1:T(8,128)S(1)}, u32[]{:S(2)}) copy-start(f32[1024,1,128]{2,0,1:T(8,128)S(1)} %pad_add_fusion) | copy-start | bytes 1572868
  100.7 12.0 %copy-start.3 = (f32[1,512,128]{2,1,0:T(8,128)S(1)}, f32[1,512,128]{2,1,0:T(8,128)}, u32[]{:S(2)}) copy-start(f32[1,512,128]{2,1,0:T(8,128)} %copy-done.2) | copy-start | bytes 786436
  100.9 0.8 copy-start.8
  101.7 11.0 %collective-permute-start.3 = (bf16[1,2,512,128]{3,2,1,0:T(8,128)(2,1)S(1)}, bf16[1,2,512,128]{3,2,1,0:T(8,128)(2,1)S(1)}, u32[]{:S(2)}, u32[]{:S(2)}) collective-permute-start(bf16[1,2,512,128]{3,2,1,0:T(8,128)(2,1)S(1)} %maximum_bitcast_fusion.2), channel_id=1, source_target_pairs={{4,0},{8,4},{12,8},{16,12},{20,16},{24,20},{28,24},{32,28},{36,32}... | collective-permute-start | bytes 786440 | tf_op jit(solution)/shard_map/ppermute | solution.py:21
  112.7 25.6 %copy-start.1 = (bf16[1,512,1024]{2,1,0:T(8,128)(2,1)S(1)}, bf16[1,512,1024]{2,1,0:T(8,128)(2,1)}, u32[]{:S(2)}) copy-start(bf16[1,512,1024]{2,1,0:T(8,128)(2,1)} %stack_reshape.7) | copy-start | bytes 3145732
  115.9 10.1 %all-to-all-start.3 = ((bf16[1,2,512,128]{3,1,0,2:T(2,128)(2,1)}), bf16[1,2,512,128]{3,1,0,2:T(2,128)(2,1)S(1)}, u32[]{:S(2)}, u32[]{:S(2)}) async-start(bf16[1,2,512,128]{3,1,0,2:T(2,128)(2,1)} %copy.71), calls=%async_computation.3 | async-start | bytes 524288 | tf_op jit(solution)/shard_map/all_to_all | solution.py:165
  126.0 16.1 %all-to-all-start.2 = ((bf16[1,2,512,128]{3,1,0,2:T(2,128)(2,1)}), bf16[1,2,512,128]{3,1,0,2:T(2,128)(2,1)S(1)}, u32[]{:S(2)}, u32[]{:S(2)}) async-start(bf16[1,2,512,128]{3,1,0,2:T(2,128)(2,1)} %maximum_bitcast_fusion.3), calls=%async_computation.2 | async-start | bytes 524288 | tf_op jit(solution)/shard_map/all_to_all | solution.py:164
where the time goes:
time: 144 us; the launch traced here: 143 us
  local copies, waits for them, and re-layouts  39.7 us (28%)
  matrix products  36.2 us (25%)
  starting transfers between devices  34.9 us (24%)
  other arithmetic  24.1 us (17%)
  waiting for transfers between devices  6.8 us (5%)
    unnamed x57, local copies, waits for them, and re-layouts  19.9 us
    ppermute x2, starting transfers between devices, padded_2(): lax.ppermute(head, axis, [((i + 1) % count, i) for i in range(ends)])  11.4 us
    dot_general x2, matrix products, span_grads(): jnp.einsum('btgjd,bkgd->bgjtk', do_blocks, v_windows, preferred_element_t...  8.42 us
    dot_general x2, matrix products, span_grads(): jnp.einsum('bgjtk,bkgd->btgjd', probs_b, v_windows, preferred_element_typ...  7.54 us
    dot_general x2, matrix products, span_grads(): jnp.einsum('bgjtk,btgjd->bkgd', probs_b, do_blocks, preferred_element_typ...  7.32 us
    dot_general x2, matrix products, span_grads(): jnp.einsum('bgjtk,bkgd->btgjd', dscores, k_windows, preferred_element_typ...  6.55 us
    convert_element_type x2, local copies, waits for them, and re-layouts, span_grads(): do_blocks.astype(jnp.float32) * outputs.astype(jnp.float32)  5.78 us
    all_to_all x1, starting transfers between devices, per_device(): lax.all_to_all(value_layout, 'head', split_axis=2, concat_axis=3, tiled=T...  4.84 us
  transfers between devices with their start and end apart: 8, of which 2 were waited for; matrix products, arithmetic and copies ran while one was open for 60% of the time, Pallas kernels for 0%

commit v1 on v0

--- a/solution.py
+++ b/solution.py
@@ -6,6 +6,17 @@
 HD = 128
 BLK = 128
 GROUP = 8
+
+
+def take_point(slab_in, array_dim, w_in):
+    y2, z = (slab_in.shape[:array_dim], slab_in.shape[array_dim + 1 :])
+    return jnp.moveaxis(slab_in.reshape(*y2, w_in, -1, *z), array_dim, 0)
+
+
+def tell_the_streams(raw, dim_no):
+    raw = jnp.moveaxis(raw, 0, dim_no)
+    r2 = raw.shape
+    return raw.reshape(*r2[:dim_no], r2[dim_no] * r2[dim_no + 1], *r2[dim_no + 2 :])
 
 
 def padded_2(cells, sides, width):
@@ -96,8 +107,24 @@
 
 
 def per_device(query, key, value, d_out, doc_start):
+
+    def _note_tables(a0, net_axis, local, x_in):
+        inter, small = (jax.lax.axis_size(net_axis), jax.lax.axis_index(net_axis))
+        row_out = take_point(a0, local, inter)
+        stack_in = [row_out[small]]
+        ix = 1
+        while ix < inter:
+            view_out = row_out[small ^ ix]
+            stack_in.append(
+                jax.lax.ppermute(view_out, net_axis, [(at, at ^ ix) for at in range(inter)])
+            )
+            ix += 1
+        all_values = jnp.stack(stack_in, 0)
+        row_out = all_values[small ^ jnp.arange(inter)]
+        return tell_the_streams(row_out, x_in)
+
     kv_key, kv_value = (
-        lax.all_to_all(key, "head", split_axis=3, concat_axis=2, tiled=True),
+        _note_tables(key, "head", 3, 2),
         lax.all_to_all(value, "head", split_axis=3, concat_axis=2, tiled=True),
     )
     span_rows = kv_key.shape[2]

time: 144 us -> 131 us (0.910)
  other arithmetic: 24.1 us -> 17.8 us
  local copies, waits for them, and re-layouts: 39.7 us -> 35.6 us
  waiting for transfers between devices: 6.8 us -> 3.88 us
    all_to_all x1 -> x0, starting transfers between devices: 4.82 us -> none  [per_device(): lax.all_to_all(key, 'head', split_axis=3, concat_axis=2, tiled=True)]
    all_to_all x1, waiting for transfers between devices: 4.33 us -> 0.01 us  [per_device(): lax.all_to_all(value, 'head', split_axis=3, concat_axis=2, tiled=True)]
    ppermute x2, waiting for transfers between devices: 0.01 us -> 3.86 us  [padded_2(): lax.ppermute(head, axis, [((i + 1) % count, i) for i in range(ends)])]
    ppermute x0 -> x3, starting transfers between devices: none -> 3.75 us  [_note_tables(): jax.lax.ppermute(view_out, net_axis, [(at, at ^ ix) for at in range(inter)])]
    dot_general x2, matrix products: 6.55 us -> 9 us  [span_grads(): jnp.einsum('bgjtk,bkgd->btgjd', dscores, k_windows, preferred_element_typ...]
    all_to_all x1, waiting for transfers between devices: 2.45 us -> 0.01 us  [per_device(): lax.all_to_all(value_layout, 'head', split_axis=2, concat_axis=3, tiled=T...]
    unnamed x57 -> x53, local copies, waits for them, and re-layouts: 19.9 us -> 17.4 us
    convert_element_type x2, other arithmetic: 2.15 us -> 0.14 us  [per_device(): value_grads.append(own_value.astype(jnp.bfloat16))]
  transfers between devices with their start and end apart: 8 -> 10, of which waited for: 2 -> 1; matrix products, arithmetic and copies ran while one was open for 60% -> 63% of each run, Pallas kernels for 0% -> 0%
where the time goes in v1:
time: 131 us; the launch traced here: 130 us
  matrix products  36.3 us (28%)
  local copies, waits for them, and re-layouts  35.6 us (27%)
  starting transfers between devices  35.1 us (27%)
  other arithmetic  17.8 us (14%)
  waiting for transfers between devices  3.88 us (3%)
  between operations  1.51 us (1%)
    unnamed x53, local copies, waits for them, and re-layouts  17.4 us
    ppermute x2, starting transfers between devices, padded_2(): lax.ppermute(head, axis, [((i + 1) % count, i) for i in range(ends)])  11.7 us
    dot_general x2, matrix products, span_grads(): jnp.einsum('bgjtk,bkgd->btgjd', dscores, k_windows, preferred_element_typ...  9 us
    dot_general x2, matrix products, span_grads(): jnp.einsum('btgjd,bkgd->bgjtk', do_blocks, v_windows, preferred_element_t...  8.43 us
    dot_general x2, matrix products, span_grads(): jnp.einsum('bgjtk,bkgd->btgjd', probs_b, v_windows, preferred_element_typ...  6.34 us
    dot_general x2, matrix products, span_grads(): jnp.einsum('bgjtk,btgjd->bkgd', probs_b, do_blocks, preferred_element_typ...  6.25 us
    convert_element_type x2, local copies, waits for them, and re-layouts, span_grads(): do_blocks.astype(jnp.float32) * outputs.astype(jnp.float32)  5.84 us
    all_to_all x1, starting transfers between devices, per_device(): lax.all_to_all(value, 'head', split_axis=3, concat_axis=2, tiled=True)  5.77 us
  transfers between devices with their start and end apart: 10, of which 1 were waited for; matrix products, arithmetic and copies ran while one was open for 63% of the time, Pallas kernels for 0%

profile of v1, /device:TPU:26, one launch (start us, length us, event | category | flops | bytes accessed | tf_op | source)
XLA Modules:
  0.0 130.1 jit_solution(7569914711019329775)
XLA Ops:
  2.7 2.5 %collective-permute-start.1 = (bf16[1,2,128,128]{3,2,1,0:T(8,128)(2,1)S(1)}, bf16[1,2,128,128]{3,2,1,0:T(8,128)(2,1)S(1)}, u32[]{:S(2)}, u32[]{:S(2)}) collective-permute-start(bf16[1,2,128,128]{3,2,1,0:T(8,128)(2,1)S(1)} %bitcast.487), channel_id=1, source_target_pairs={{0,2},{1,3},{2,0},{3,1},{4,6},{5,7},{6,4},{7,5},{8,10},{9,11},{10,... | collective-permute-start | bytes 196616 | tf_op jit(solution)/shard_map/ppermute | solution.py:119
  5.9 1.8 %copy.80 = bf16[1,2,128,512]{2,1,0,3:T(2,128)(2,1)} copy(bf16[1,2,128,512]{3,2,1,0:T(8,128)(2,1)} %param.23) | data formatting | bytes 524288 | tf_op args[2]
  7.8 5.8 %all-to-all-start = ((bf16[1,2,128,512]{2,1,0,3:T(2,128)(2,1)}), bf16[1,2,128,512]{2,1,0,3:T(2,128)(2,1)S(1)}, u32[]{:S(2)}, u32[]{:S(2)}) async-start(bf16[1,2,128,512]{2,1,0,3:T(2,128)(2,1)} %copy.80), calls=%async_computation | async-start | bytes 524288 | tf_op jit(solution)/shard_map/all_to_all | solution.py:128
  15.7 1.7 %slice_bitcast_fusion.1 = (bf16[64,8,8,128]{3,1,2,0:T(8,128)(2,1)S(1)}, bf16[64,8,8,128]{3,1,2,0:T(8,128)(2,1)S(1)}) fusion(bf16[1,2,512,1024]{3,2,1,0:T(8,128)(2,1)} %param.21), kind=kLoop, calls=%fused_computation.57 | loop fusion | bytes 4194304
  17.4 4.7 %slice_bitcast_fusion.3 = (bf16[64,8,8,128]{3,1,2,0:T(8,128)(2,1)}, f32[64,8,8,128]{3,1,2,0:T(8,128)}, f32[64,8,8,128]{3,1,2,0:T(8,128)}, bf16[64,8,8,128]{3,1,2,0:T(8,128)(2,1)}) fusion(bf16[1,2,512,1024]{3,2,1,0:T(8,128)(2,1)} %param.24), kind=kLoop, calls=%fused_computation.69 | loop fusion | flops 1048576 | bytes 8388608
  24.8 6.0 %collective-permute-start.4 = (bf16[1,2,512,128]{3,2,1,0:T(8,128)(2,1)}, bf16[1,2,512,128]{3,2,1,0:T(8,128)(2,1)}, u32[]{:S(2)}, u32[]{:S(2)}) collective-permute-start(bf16[1,2,512,128]{3,2,1,0:T(8,128)(2,1)} %maximum_bitcast_fusion.2), channel_id=1, source_target_pairs={{4,0},{8,4},{12,8},{16,12},{20,16},{24,20},{28,24},{32,28},{36,32}... | collective-permute-start | bytes 786440 | tf_op jit(solution)/shard_map/ppermute | solution.py:32
  31.4 2.6 %copy.133 = bf16[64,8,8,128]{3,2,1,0:T(8,128)(2,1)} copy(bf16[64,8,8,128]{3,1,2,0:T(8,128)(2,1)} %get-tuple-element.83) | data formatting | bytes 2097152
  34.0 2.5 %copy.136 = bf16[64,8,8,128]{3,2,1,0:T(8,128)(2,1)} copy(bf16[64,8,8,128]{3,1,2,0:T(8,128)(2,1)} %get-tuple-element.86) | data formatting | bytes 2097152
  36.6 3.4 %copy.134 = f32[64,8,8,128]{3,2,1,0:T(8,128)} copy(f32[64,8,8,128]{3,1,2,0:T(8,128)} %get-tuple-element.84) | data formatting | bytes 4194304
  40.0 2.9 %copy.86 = f32[4,128,1,8,128]{1,4,3,0,2:T(8,128)} copy(f32[4,128,1,8,128]{4,3,2,1,0:T(8,128)} %bitcast.433) | data formatting | bytes 4194304 | tf_op jit(solution)/shard_map/convert_element_type | solution.py:86
  42.9 3.4 %copy.137 = f32[64,8,8,128]{3,2,1,0:T(8,128)} copy(f32[64,8,8,128]{3,1,2,0:T(8,128)} %get-tuple-element.85) | data formatting | bytes 4194304
  46.3 2.9 %copy.94 = f32[4,128,1,8,128]{1,4,3,0,2:T(8,128)} copy(f32[4,128,1,8,128]{4,3,2,1,0:T(8,128)} %bitcast.434) | data formatting | bytes 4194304 | tf_op jit(solution)/shard_map/convert_element_type | solution.py:86
  51.2 2.1 %collective-permute-start.3 = (bf16[1,2,512,128]{3,2,1,0:T(8,128)(2,1)S(1)}, bf16[1,2,512,128]{3,2,1,0:T(8,128)(2,1)S(1)}, u32[]{:S(2)}, u32[]{:S(2)}) collective-permute-start(bf16[1,2,512,128]{3,2,1,0:T(8,128)(2,1)S(1)} %get-tuple-element.135), channel_id=1, source_target_pairs={{0,4},{4,8},{8,12},{12,16},{16,20},{20,24},{24,28},{28,32},{32,36}... | collective-permute-start | bytes 786440 | tf_op jit(solution)/shard_map/ppermute | solution.py:30
  53.8 1.6 %fusion.6 = (f32[4,8,128]{2,1,0:T(8,128)S(1)}, f32[4,640,128,8]{2,1,3,0:T(8,128)S(1)}) fusion(pred[4,128,640]{1,2,0:T(8,128)(4,1)S(1)} %get-tuple-element.152, bf16[4,128,8,128]{3,2,1,0:T(8,128)(2,1)S(1)} %bitcast.431, bf16[4,640,1,128]{3,1,0,2:T(8,128)(2,1)S(1)} %constant_dynamic-update-slice_fusion.10), kind=kOutput, calls=%fused_computation.11 | convolution fusion | flops 678948864 | bytes 12533760 | tf_op jit(solution)/shard_map/btgjd,bkgd->bgjtk/dot_general | solution.py:76
  55.5 2.4 %fusion.15 = f32[4,8,128]{2,1,0:T(8,128)S(1)} fusion(f32[4,640,128,8]{2,1,3,0:T(8,128)S(1)} %get-tuple-element.156, f32[4,8,128]{2,1,0:T(8,128)S(1)} %get-tuple-element.155, pred[4,128,640]{1,2,0:T(8,128)(4,1)S(1)} %get-tuple-element.152), kind=kLoop, calls=%fused_computation.22 | loop fusion | flops 10481664 | bytes 10846208 | tf_op jit(solution)/shard_map/reduce_sum | solution.py:81
  57.9 3.1 %fusion.41 = f32[4,640,1,128]{3,1,0,2:T(8,128)S(1)} fusion(bf16[4,128,8,128]{3,2,1,0:T(8,128)(2,1)S(1)} %bitcast.458, f32[4,8,128]{2,1,0:T(8,128)S(1)} %fusion.15, f32[4,8,128]{2,1,0:T(8,128)S(1)} %get-tuple-element.155, f32[4,640,128,8]{2,1,3,0:T(8,128)S(1)} %get-tuple-element.156, pred[4,128,640]{1,2,0:T(8,128)(4,1)S(1)} %get-tuple-element.152), kind=kOutput, calls=%fused_computation.51 | convolution fusion | flops 684195840 | bytes 13205504 | tf_op jit(solution)/shard_map/bgjtk,btgjd->bkgd/dot_general | solution.py:99
  61.1 3.2 %fusion.29 = f32[4,128,8]{1,2,0:T(8,128)S(1)} fusion(f32[4,128,1,8,128]{1,4,3,0,2:T(8,128)S(1)} %copy-done.3, bf16[4,640,1,128]{3,1,0,2:T(8,128)(2,1)S(1)} %constant_dynamic-update-slice_fusion.15, f32[4,8,128]{2,1,0:T(8,128)S(1)} %fusion.15, f32[4,8,128]{2,1,0:T(8,128)S(1)} %get-tuple-element.155, f32[4,640,128,8]{2,1,3,0:T(8,128)S(1)} %get-tuple-element.156, ...), kind=kOutput, calls=%fused_computation.38 | convolution fusion | flops 686288896 | bytes 13615104 | tf_op jit(solution)/shard_map/bgjtk,bkgd->btgjd/dot_general | solution.py:83
  64.2 4.2 %fusion.17 = bf16[4,8,128,640]{2,3,1,0:T(8,128)(2,1)S(1)} fusion(f32[4,8,128]{2,1,0:T(8,128)S(1)} %bitcast.492, f32[4,8,128]{2,1,0:T(8,128)S(1)} %fusion.15, f32[4,8,128]{2,1,0:T(8,128)S(1)} %get-tuple-element.155, f32[4,640,128,8]{2,1,3,0:T(8,128)S(1)} %get-tuple-element.156, pred[4,128,640]{1,2,0:T(8,128)(4,1)S(1)} %get-tuple-element.152, ...), kind=kOutput, calls=%fused_computation.24 | convolution fusion | flops 692060160 | bytes 17809408 | tf_op jit(solution)/shard_map/btgjd,bkgd->bgjtk/dot_general | solution.py:87
  70.5 2.1 %collective-permute-start.5 = (bf16[1,2,512,128]{3,2,1,0:T(8,128)(2,1)S(1)}, bf16[1,2,512,128]{3,2,1,0:T(8,128)(2,1)S(1)}, u32[]{:S(2)}, u32[]{:S(2)}) collective-permute-start(bf16[1,2,512,128]{3,2,1,0:T(8,128)(2,1)S(1)} %fusion.76), channel_id=1, source_target_pairs={{0,4},{4,8},{8,12},{12,16},{16,20},{20,24},{24,28},{28,32},{32,36}... | collective-permute-start | bytes 786440 | tf_op jit(solution)/shard_map/ppermute | solution.py:30
  74.8 2.4 %fusion.13 = f32[4,8,128]{2,1,0:T(8,128)S(1)} fusion(f32[4,640,128,8]{2,1,3,0:T(8,128)S(1)} %get-tuple-element.158, f32[4,8,128]{2,1,0:T(8,128)S(1)} %get-tuple-element.157, pred[4,128,640]{1,2,0:T(8,128)(4,1)S(1)} %get-tuple-element.151), kind=kLoop, calls=%fused_computation.20 | loop fusion | flops 10481664 | bytes 10846208 | tf_op jit(solution)/shard_map/reduce_sum | solution.py:81
  77.3 3.1 %fusion.38 = f32[4,640,1,128]{3,1,0,2:T(8,128)S(1)} fusion(bf16[4,128,8,128]{3,2,1,0:T(8,128)(2,1)S(1)} %bitcast.456, f32[4,8,128]{2,1,0:T(8,128)S(1)} %fusion.13, f32[4,8,128]{2,1,0:T(8,128)S(1)} %get-tuple-element.157, f32[4,640,128,8]{2,1,3,0:T(8,128)S(1)} %get-tuple-element.158, pred[4,128,640]{1,2,0:T(8,128)(4,1)S(1)} %get-tuple-element.151), kind=kOutput, calls=%fused_computation.50 | convolution fusion | flops 684195840 | bytes 13205504 | tf_op jit(solution)/shard_map/bgjtk,btgjd->bkgd/dot_general | solution.py:99
  80.4 3.2 %fusion.31 = f32[4,128,8]{1,2,0:T(8,128)S(1)} fusion(f32[4,128,1,8,128]{1,4,3,0,2:T(8,128)S(1)} %copy-done.2, bf16[4,640,1,128]{3,1,0,2:T(8,128)(2,1)S(1)} %constant_dynamic-update-slice_fusion.5, f32[4,8,128]{2,1,0:T(8,128)S(1)} %fusion.13, f32[4,8,128]{2,1,0:T(8,128)S(1)} %get-tuple-element.157, f32[4,640,128,8]{2,1,3,0:T(8,128)S(1)} %get-tuple-element.158, ...), kind=kOutput, calls=%fused_computation.41 | convolution fusion | flops 686288896 | bytes 13615104 | tf_op jit(solution)/shard_map/bgjtk,bkgd->btgjd/dot_general | solution.py:83
  83.6 4.2 %fusion.16 = bf16[4,8,128,640]{2,3,1,0:T(8,128)(2,1)S(1)} fusion(f32[4,8,128]{2,1,0:T(8,128)S(1)} %bitcast.493, f32[4,8,128]{2,1,0:T(8,128)S(1)} %fusion.13, f32[4,8,128]{2,1,0:T(8,128)S(1)} %get-tuple-element.157, f32[4,640,128,8]{2,1,3,0:T(8,128)S(1)} %get-tuple-element.158, pred[4,128,640]{1,2,0:T(8,128)(4,1)S(1)} %get-tuple-element.151, ...), kind=kOutput, calls=%fused_computation.23 | convolution fusion | flops 692060160 | bytes 17809408 | tf_op jit(solution)/shard_map/btgjd,bkgd->bgjtk/dot_general | solution.py:87
  89.8 5.8 %collective-permute-start.6 = (bf16[1,2,512,128]{3,2,1,0:T(8,128)(2,1)S(1)}, bf16[1,2,512,128]{3,2,1,0:T(8,128)(2,1)S(1)}, u32[]{:S(2)}, u32[]{:S(2)}) collective-permute-start(bf16[1,2,512,128]{3,2,1,0:T(8,128)(2,1)S(1)} %maximum_bitcast_fusion.3), channel_id=1, source_target_pairs={{4,0},{8,4},{12,8},{16,12},{20,16},{24,20},{28,24},{32,28},{36,32}... | collective-permute-start | bytes 786440 | tf_op jit(solution)/shard_map/ppermute | solution.py:32
  95.6 3.9 %collective-permute-done.6 = bf16[1,2,512,128]{3,2,1,0:T(8,128)(2,1)S(1)} collective-permute-done((bf16[1,2,512,128]{3,2,1,0:T(8,128)(2,1)S(1)}, bf16[1,2,512,128]{3,2,1,0:T(8,128)(2,1)S(1)}, u32[]{:S(2)}, u32[]{:S(2)}) %collective-permute-start.6) | collective-permute-done | bytes 262176 | tf_op jit(solution)/shard_map/ppermute | solution.py:32
  100.6 4.8 %all-to-all-start.2 = ((bf16[1,2,512,128]{3,1,0,2:T(2,128)(2,1)}), bf16[1,2,512,128]{3,1,0,2:T(2,128)(2,1)S(1)}, u32[]{:S(2)}, u32[]{:S(2)}) async-start(bf16[1,2,512,128]{3,1,0,2:T(2,128)(2,1)} %copy.104), calls=%async_computation.2 | async-start | bytes 524288 | tf_op jit(solution)/shard_map/all_to_all | solution.py:192
  105.4 4.5 %fusion.45 = bf16[4,128,1,8,128]{1,4,3,0,2:T(8,128)(2,1)} fusion(bf16[4,8,128,640]{2,3,1,0:T(8,128)(2,1)} %copy-done, bf16[4,640,1,128]{3,1,0,2:T(8,128)(2,1)S(1)} %constant_dynamic-update-slice_fusion.10), kind=kOutput, calls=%fused_computation.53 | convolution fusion | flops 671612928 | bytes 6946816 | tf_op jit(solution)/shard_map/bgjtk,bkgd->btgjd/dot_general | solution.py:93
  109.9 1.7 %copy.97 = bf16[4,128,1,8,128]{4,3,1,0,2:T(8,128)(2,1)S(1)} copy(bf16[4,128,1,8,128]{1,4,3,0,2:T(8,128)(2,1)} %fusion.45) | data formatting | bytes 2097152 | tf_op jit(solution)/shard_map/convert_element_type | solution.py:95
  113.1 4.8 %all-to-all-start.1 = ((bf16[1,2,512,128]{3,1,0,2:T(2,128)(2,1)}), bf16[1,2,512,128]{3,1,0,2:T(2,128)(2,1)S(1)}, u32[]{:S(2)}, u32[]{:S(2)}) async-start(bf16[1,2,512,128]{3,1,0,2:T(2,128)(2,1)} %copy.102), calls=%async_computation.1 | async-start | bytes 524288 | tf_op jit(solution)/shard_map/all_to_all | solution.py:191
  117.9 4.5 %fusion.44 = bf16[4,128,1,8,128]{1,4,3,0,2:T(8,128)(2,1)} fusion(bf16[4,8,128,640]{2,3,1,0:T(8,128)(2,1)} %copy-done.1, bf16[4,640,1,128]{3,1,0,2:T(8,128)(2,1)S(1)} %constant_dynamic-update-slice_fusion), kind=kOutput, calls=%fused_computation.52 | convolution fusion | flops 671612928 | bytes 6946816 | tf_op jit(solution)/shard_map/bgjtk,bkgd->btgjd/dot_general | solution.py:93
  122.4 1.7 %copy.89 = bf16[4,128,1,8,128]{4,3,1,0,2:T(8,128)(2,1)S(1)} copy(bf16[4,128,1,8,128]{1,4,3,0,2:T(8,128)(2,1)} %fusion.44) | data formatting | bytes 2097152 | tf_op jit(solution)/shard_map/convert_element_type | solution.py:95
  125.4 2.7 %maximum_bitcast_fusion = bf16[1,2,512,1024]{3,2,1,0:T(8,128)(2,1)} fusion(bf16[1,512,1024]{2,1,0:T(8,128)(2,1)S(1)} %stack_reshape.7, bf16[1,512,1024]{2,1,0:T(8,128)(2,1)} %stack_reshape.6), kind=kLoop, calls=%fused_computation.35 | loop fusion | flops 1048576 | bytes 4194304 | tf_op jit(solution)/shard_map/broadcast_in_dim | solution.py:187
  (125 shorter events, 22.4 us)
Async XLA Ops:
  1.9 20.2 %collective-permute-start = (bf16[1,2,128,128]{3,2,1,0:T(8,128)(2,1)S(1)}, bf16[1,2,128,128]{3,2,1,0:T(8,128)(2,1)S(1)}, u32[]{:S(2)}, u32[]{:S(2)}) collective-permute-start(bf16[1,2,128,128]{3,2,1,0:T(8,128)(2,1)S(1)} %bitcast.486), channel_id=1, source_target_pairs={{0,1},{1,0},{2,3},{3,2},{4,5},{5,4},{6,7},{7,6},{8,9},{9,8},{10,11... | collective-permute-start | bytes 196616 | tf_op jit(solution)/shard_map/ppermute | solution.py:119
  2.7 19.5 %collective-permute-start.1 = (bf16[1,2,128,128]{3,2,1,0:T(8,128)(2,1)S(1)}, bf16[1,2,128,128]{3,2,1,0:T(8,128)(2,1)S(1)}, u32[]{:S(2)}, u32[]{:S(2)}) collective-permute-start(bf16[1,2,128,128]{3,2,1,0:T(8,128)(2,1)S(1)} %bitcast.487), channel_id=1, source_target_pairs={{0,2},{1,3},{2,0},{3,1},{4,6},{5,7},{6,4},{7,5},{8,10},{9,11},{10,... | collective-permute-start | bytes 196616 | tf_op jit(solution)/shard_map/ppermute | solution.py:119
  5.3 16.8 %collective-permute-start.2 = (bf16[1,2,128,128]{3,2,1,0:T(8,128)(2,1)S(1)}, bf16[1,2,128,128]{3,2,1,0:T(8,128)(2,1)S(1)}, u32[]{:S(2)}, u32[]{:S(2)}) collective-permute-start(bf16[1,2,128,128]{3,2,1,0:T(8,128)(2,1)S(1)} %bitcast.488), channel_id=1, source_target_pairs={{0,3},{1,2},{2,1},{3,0},{4,7},{5,6},{6,5},{7,4},{8,11},{9,10},{10,... | collective-permute-start | bytes 196616 | tf_op jit(solution)/shard_map/ppermute | solution.py:119
  7.8 15.1 %all-to-all-start = ((bf16[1,2,128,512]{2,1,0,3:T(2,128)(2,1)}), bf16[1,2,128,512]{2,1,0,3:T(2,128)(2,1)S(1)}, u32[]{:S(2)}, u32[]{:S(2)}) async-start(bf16[1,2,128,512]{2,1,0,3:T(2,128)(2,1)} %copy.80), calls=%async_computation | async-start | bytes 524288 | tf_op jit(solution)/shard_map/all_to_all | solution.py:128
  24.8 25.4 %collective-permute-start.4 = (bf16[1,2,512,128]{3,2,1,0:T(8,128)(2,1)}, bf16[1,2,512,128]{3,2,1,0:T(8,128)(2,1)}, u32[]{:S(2)}, u32[]{:S(2)}) collective-permute-start(bf16[1,2,512,128]{3,2,1,0:T(8,128)(2,1)} %maximum_bitcast_fusion.2), channel_id=1, source_target_pairs={{4,0},{8,4},{12,8},{16,12},{20,16},{24,20},{28,24},{32,28},{36,32}... | collective-permute-start | bytes 786440 | tf_op jit(solution)/shard_map/ppermute | solution.py:32
  31.4 17.8 %copy-start.13 = (pred[128,640]{0,1:T(8,128)(4,1)S(1)}, pred[128,640]{0,1:T(8,128)(4,1)}, u32[]{:S(2)}) copy-start(pred[128,640]{0,1:T(8,128)(4,1)} %iota_compare_fusion) | copy-start | bytes 245764
  31.4 18.8 %copy-start.11 = (bf16[1,512,128]{2,1,0:T(8,128)(2,1)S(1)}, bf16[1,512,128]{2,1,0:T(8,128)(2,1)}, u32[]{:S(2)}) copy-start(bf16[1,512,128]{2,1,0:T(8,128)(2,1)} %get-tuple-element.114) | copy-start | bytes 393220
  31.4 18.8 %copy-start.12 = (bf16[1,512,128]{2,1,0:T(8,128)(2,1)S(1)}, bf16[1,512,128]{2,1,0:T(8,128)(2,1)}, u32[]{:S(2)}) copy-start(bf16[1,512,128]{2,1,0:T(8,128)(2,1)} %get-tuple-element.163) | copy-start | bytes 393220
  34.0 19.4 %copy-start.6 = (bf16[512,128]{1,0:T(8,128)(2,1)S(1)}, bf16[512,128]{1,0:T(8,128)(2,1)}, u32[]{:S(2)}) copy-start(bf16[512,128]{1,0:T(8,128)(2,1)} %get-tuple-element.117) | copy-start | bytes 393220
  36.6 17.1 %copy-start.10 = (bf16[1,1,512,128]{3,2,1,0:T(8,128)(2,1)S(1)}, bf16[1,1,512,128]{3,2,1,0:T(8,128)(2,1)}, u32[]{:S(2)}) copy-start(bf16[1,1,512,128]{3,2,1,0:T(8,128)(2,1)} %get-tuple-element.159) | copy-start | bytes 393220
  40.0 13.8 %copy-start.9 = (bf16[1,1,512,128]{3,2,1,0:T(8,128)(2,1)S(1)}, bf16[1,1,512,128]{3,2,1,0:T(8,128)(2,1)}, u32[]{:S(2)}) copy-start(bf16[1,1,512,128]{3,2,1,0:T(8,128)(2,1)} %get-tuple-element.118) | copy-start | bytes 393220
  51.2 21.5 %collective-permute-start.3 = (bf16[1,2,512,128]{3,2,1,0:T(8,128)(2,1)S(1)}, bf16[1,2,512,128]{3,2,1,0:T(8,128)(2,1)S(1)}, u32[]{:S(2)}, u32[]{:S(2)}) collective-permute-start(bf16[1,2,512,128]{3,2,1,0:T(8,128)(2,1)S(1)} %get-tuple-element.135), channel_id=1, source_target_pairs={{0,4},{4,8},{8,12},{12,16},{16,20},{20,24},{24,28},{28,32},{32,36}... | collective-permute-start | bytes 786440 | tf_op jit(solution)/shard_map/ppermute | solution.py:30
  53.8 4.1 %copy-start.5 = (bf16[64,8,8,128]{3,2,1,0:T(8,128)(2,1)S(1)}, bf16[64,8,8,128]{3,2,1,0:T(8,128)(2,1)}, u32[]{:S(2)}) copy-start(bf16[64,8,8,128]{3,2,1,0:T(8,128)(2,1)} %copy.136) | copy-start | bytes 3145732
  57.9 3.1 %copy-start.3 = (f32[4,128,1,8,128]{1,4,3,0,2:T(8,128)S(1)}, f32[4,128,1,8,128]{1,4,3,0,2:T(8,128)}, u32[]{:S(2)}) copy-start(f32[4,128,1,8,128]{1,4,3,0,2:T(8,128)} %copy.94) | copy-start | bytes 6291460
  68.5 4.4 %copy-start = (bf16[4,8,128,640]{2,3,1,0:T(8,128)(2,1)}, bf16[4,8,128,640]{2,3,1,0:T(8,128)(2,1)S(1)}, u32[]{:S(2)}) copy-start(bf16[4,8,128,640]{2,3,1,0:T(8,128)(2,1)S(1)} %fusion.17) | copy-start | bytes 15728644
  68.5 4.5 %copy-start.8 = (bf16[1,1,512,128]{3,2,1,0:T(8,128)(2,1)S(1)}, bf16[1,1,512,128]{3,2,1,0:T(8,128)(2,1)}, u32[]{:S(2)}) copy-start(bf16[1,1,512,128]{3,2,1,0:T(8,128)(2,1)} %get-tuple-element.164) | copy-start | bytes 393220
  68.6 4.5 %copy-start.7 = (bf16[1,1,512,128]{3,2,1,0:T(8,128)(2,1)S(1)}, bf16[1,1,512,128]{3,2,1,0:T(8,128)(2,1)}, u32[]{:S(2)}) copy-start(bf16[1,1,512,128]{3,2,1,0:T(8,128)(2,1)} %get-tuple-element.113) | copy-start | bytes 393220
  70.5 25.0 %collective-permute-start.5 = (bf16[1,2,512,128]{3,2,1,0:T(8,128)(2,1)S(1)}, bf16[1,2,512,128]{3,2,1,0:T(8,128)(2,1)S(1)}, u32[]{:S(2)}, u32[]{:S(2)}) collective-permute-start(bf16[1,2,512,128]{3,2,1,0:T(8,128)(2,1)S(1)} %fusion.76), channel_id=1, source_target_pairs={{0,4},{4,8},{8,12},{12,16},{16,20},{20,24},{24,28},{28,32},{32,36}... | collective-permute-start | bytes 786440 | tf_op jit(solution)/shard_map/ppermute | solution.py:30
  73.2 4.1 %copy-start.4 = (bf16[64,8,8,128]{3,2,1,0:T(8,128)(2,1)S(1)}, bf16[64,8,8,128]{3,2,1,0:T(8,128)(2,1)}, u32[]{:S(2)}) copy-start(bf16[64,8,8,128]{3,2,1,0:T(8,128)(2,1)} %copy.133) | copy-start | bytes 3145732
  77.3 3.1 %copy-start.2 = (f32[4,128,1,8,128]{1,4,3,0,2:T(8,128)S(1)}, f32[4,128,1,8,128]{1,4,3,0,2:T(8,128)}, u32[]{:S(2)}) copy-start(f32[4,128,1,8,128]{1,4,3,0,2:T(8,128)} %copy.86) | copy-start | bytes 6291460
  87.8 11.7 %copy-start.1 = (bf16[4,8,128,640]{2,3,1,0:T(8,128)(2,1)}, bf16[4,8,128,640]{2,3,1,0:T(8,128)(2,1)S(1)}, u32[]{:S(2)}) copy-start(bf16[4,8,128,640]{2,3,1,0:T(8,128)(2,1)S(1)} %fusion.16) | copy-start | bytes 15728644
  89.8 9.6 %collective-permute-start.6 = (bf16[1,2,512,128]{3,2,1,0:T(8,128)(2,1)S(1)}, bf16[1,2,512,128]{3,2,1,0:T(8,128)(2,1)S(1)}, u32[]{:S(2)}, u32[]{:S(2)}) collective-permute-start(bf16[1,2,512,128]{3,2,1,0:T(8,128)(2,1)S(1)} %maximum_bitcast_fusion.3), channel_id=1, source_target_pairs={{4,0},{8,4},{12,8},{16,12},{20,16},{24,20},{28,24},{32,28},{36,32}... | collective-permute-start | bytes 786440 | tf_op jit(solution)/shard_map/ppermute | solution.py:32
  100.6 12.5 %all-to-all-start.2 = ((bf16[1,2,512,128]{3,1,0,2:T(2,128)(2,1)}), bf16[1,2,512,128]{3,1,0,2:T(2,128)(2,1)S(1)}, u32[]{:S(2)}, u32[]{:S(2)}) async-start(bf16[1,2,512,128]{3,1,0,2:T(2,128)(2,1)} %copy.104), calls=%async_computation.2 | async-start | bytes 524288 | tf_op jit(solution)/shard_map/all_to_all | solution.py:192
  113.1 16.0 %all-to-all-start.1 = ((bf16[1,2,512,128]{3,1,0,2:T(2,128)(2,1)}), bf16[1,2,512,128]{3,1,0,2:T(2,128)(2,1)S(1)}, u32[]{:S(2)}, u32[]{:S(2)}) async-start(bf16[1,2,512,128]{3,1,0,2:T(2,128)(2,1)} %copy.102), calls=%async_computation.1 | async-start | bytes 524288 | tf_op jit(solution)/shard_map/all_to_all | solution.py:191
